TPU v7x, 32 devices: a whole 2x2x4 slice. The times are simulated.
32 devices in a mesh: grp: 2 (over y), seq: 4 (over z), head: 4 (over x, core).
Axes of the slice: x: 2, y: 2, z: 4, core: 2. Of those that a mesh axis runs over, the one named last changes fastest.
Arguments:
- encoder: bfloat16 [8, 256, 4096], P('grp', 'seq'), parts along dimension 0, may hold values from -6 to 6
- key_weight: bfloat16 [4096, 4096], P('seq', 'head'), may hold values from -0.09375 to 0.09375
- value_weight: bfloat16 [4096, 4096], P('seq', 'head'), may hold values from -0.09375 to 0.09375
- tile_mask: int32 [2, 64, 64], P(None, 'seq', 'head'), may hold values 0 or 1
- lengths: int32 [8], P('grp'), parts along dimension 0, may hold values from 64 to 256, as said below
- queries: bfloat16 [8, 64, 4096], P('grp', 'seq', 'head'), parts along dimension 0, may hold values from -240 to 240
- cotangent: bfloat16 [8, 64, 4096], P('grp', 'seq', 'head'), parts along dimension 0, may hold values from -6 to 6
Outputs:
- attention: bfloat16 [8, 64, 4096], P('grp', 'seq', 'head'), parts along dimension 0
- query_grad: bfloat16 [8, 64, 4096], P('grp', 'seq', 'head'), parts along dimension 0
- encoder_grad: bfloat16 [8, 256, 4096], P('grp', 'seq', 'head'), parts along dimension 0
There are 2 independent parts, one for each index of `grp`. A program takes and returns all parts, laid end to end along the dimension named above; an argument that names none is the same for every part. Nothing has to cross between parts.
Inputs may be any that keep to these rules, and one draw needn't show every extreme that they name: `lengths`: one document of each group has all 256 positions valid.
All inputs are finite; a program needn't handle non-finite values. No bound on the sum of `tile_mask` on one device may be relied on, other than what follows from the above.
Results may differ from a plain program's by a relative error of at most 0.0096.
Values may be sent and summed in bfloat16 or wider, within the bound.
No kernel may reach another device: no remote copies, remote signals or barrier semaphores. Data moves between devices by JAX's collectives and lax.ppermute only.
A program may use at most 128 MiB of HBM per device.

v0:
```python
import jax
import jax.numpy as jnp
from jax import lax
from jax.sharding import PartitionSpec as P

DH = 64
TILE = 64
DOCS = 4
SCALE = 0.125
FLOOR_SCORE = -1e30


def expand(tile_grid, tile_edge):
    return jnp.repeat(jnp.repeat(tile_grid, tile_edge, axis=0), tile_edge, axis=1)


def attend(keys, values, queries, cotangent, length):
    position = jnp.arange(keys.shape[0])[None, :]
    live = position < length
    scores = jnp.dot(queries, keys.T, preferred_element_type=jnp.float32) * SCALE
    scores = jnp.where(live, scores, FLOOR_SCORE)
    row_max = jnp.max(scores, axis=1, keepdims=True)
    weights = jnp.where(live, jnp.exp(scores - row_max), 0.0)
    probs = weights / jnp.sum(weights, axis=1, keepdims=True)
    probs_low = probs.astype(jnp.bfloat16)
    output = jnp.dot(probs_low, values, preferred_element_type=jnp.float32)
    delta = jnp.sum(cotangent.astype(jnp.float32) * output, axis=1, keepdims=True)
    prob_grad = jnp.dot(cotangent, values.T, preferred_element_type=jnp.float32)
    score_grad = (probs * (prob_grad - delta) * SCALE).astype(jnp.bfloat16)
    query_grad = jnp.dot(score_grad, keys, preferred_element_type=jnp.float32)
    key_grad = jnp.dot(score_grad.T, queries, preferred_element_type=jnp.float32)
    value_grad = jnp.dot(probs_low.T, cotangent, preferred_element_type=jnp.float32)
    return (
        output.astype(jnp.bfloat16),
        query_grad.astype(jnp.bfloat16),
        key_grad.astype(jnp.bfloat16),
        value_grad.astype(jnp.bfloat16),
    )


def project(encoder, key_piece, value_piece):
    count = key_piece.shape[0]
    flat = encoder.reshape(DOCS * encoder.shape[1], count)
    key_flat = jnp.dot(flat, key_piece, preferred_element_type=jnp.float32)
    value_flat = jnp.dot(flat, value_piece, preferred_element_type=jnp.float32)
    shape_out = (DOCS, encoder.shape[1], key_piece.shape[1])
    return (key_flat.reshape(shape_out), value_flat.reshape(shape_out))


def back_product(key_rows, value_rows, key_piece, value_piece):
    contract = (((1,), (1,)), ((), ()))
    total = lax.dot_general(key_rows, key_piece, contract, preferred_element_type=jnp.float32)
    return total + lax.dot_general(
        value_rows, value_piece, contract, preferred_element_type=jnp.float32
    )


def body(encoder, key_weight, value_weight, tile_mask, lengths, queries, cotangent):
    seq_count = lax.axis_size("seq")
    enc_rows = encoder.shape[1]
    dec_rows = queries.shape[1]
    group_heads = queries.shape[2] // DH
    pair_count = DOCS * group_heads
    local_pairs = pair_count // seq_count
    key_masked = key_weight * expand(tile_mask[0], TILE).astype(jnp.bfloat16)
    value_masked = value_weight * expand(tile_mask[1], TILE).astype(jnp.bfloat16)
    full_key, full_value = (
        lax.all_gather(key_masked, "seq", axis=0, tiled=True),
        lax.all_gather(value_masked, "seq", axis=0, tiled=True),
    )
    key_sum, value_sum = project(encoder, full_key, full_value)

    def to_pairs(first, second, rows):
        joined = jnp.concatenate(
            [
                first.reshape(DOCS, rows, group_heads, DH),
                second.reshape(DOCS, rows, group_heads, DH),
            ],
            axis=3,
        )
        return joined.transpose(0, 2, 1, 3).reshape(pair_count, rows, 2 * DH)

    def from_pairs(block, rows):
        shaped = block.reshape(DOCS, group_heads, rows, 2 * DH).transpose(0, 2, 1, 3)
        first = shaped[..., :DH].reshape(DOCS, rows, group_heads * DH)
        second = shaped[..., DH:].reshape(DOCS, rows, group_heads * DH)
        return (first, second)

    query_pairs = to_pairs(queries, cotangent, dec_rows)
    query_owned = lax.all_to_all(query_pairs, "seq", split_axis=0, concat_axis=1, tiled=True)
    kv_pairs = to_pairs(key_sum.astype(jnp.bfloat16), value_sum.astype(jnp.bfloat16), enc_rows)
    kv_owned = lax.all_to_all(kv_pairs, "seq", split_axis=0, concat_axis=1, tiled=True)
    pair_ids = lax.axis_index("seq") * local_pairs + jnp.arange(local_pairs)
    doc_of_pair = pair_ids // group_heads
    pair_length = jnp.sum(
        jnp.where(doc_of_pair[:, None] == jnp.arange(DOCS)[None, :], lengths[None, :], 0), axis=1
    )

    def owner_pair(items):
        pair_kv, pair_query, length = items
        output, query_grad, key_grad, value_grad = attend(
            pair_kv[:, :DH], pair_kv[:, DH:], pair_query[:, :DH], pair_query[:, DH:], length
        )
        return (
            jnp.concatenate([output, query_grad], axis=1),
            jnp.concatenate([key_grad, value_grad], axis=1),
        )

    front, back = lax.map(owner_pair, (kv_owned, query_owned, pair_length))
    front_rows, back_rows = (
        lax.all_to_all(front, "seq", split_axis=1, concat_axis=0, tiled=True),
        lax.all_to_all(back, "seq", split_axis=1, concat_axis=0, tiled=True),
    )
    attention, query_grad = from_pairs(front_rows, dec_rows)
    key_grads, value_grads = from_pairs(back_rows, enc_rows)
    key_rows = key_grads.reshape(DOCS * enc_rows, group_heads * DH)
    value_rows = value_grads.reshape(DOCS * enc_rows, group_heads * DH)
    grad_terms = back_product(key_rows, value_rows, full_key, full_value)
    grad_share = lax.psum_scatter(grad_terms, "head", scatter_dimension=1, tiled=True)
    encoder_grad = grad_share.astype(jnp.bfloat16).reshape(DOCS, enc_rows, grad_share.shape[1])
    return (attention, query_grad, encoder_grad)


def solution(mesh):
    placed = (
        P("grp", "seq", None),
        P("seq", "head"),
        P("seq", "head"),
        P(None, "seq", "head"),
        P("grp"),
        P("grp", "seq", "head"),
        P("grp", "seq", "head"),
    )
    return jax.shard_map(
        body,
        mesh=mesh,
        in_specs=placed,
        out_specs=(P("grp", "seq", "head"), P("grp", "seq", "head"), P("grp", "seq", "head")),
        check_vma=False,
    )
```

profile of v0, /device:TPU:0, one launch (start us, length us, event | category | flops | bytes accessed | tf_op | source)
XLA Modules:
  0.0 557.6 jit_solution(13570915106982386981)
XLA Ops:
  7.2 0.9 convert.4
  8.4 3.9 copy.49
  12.3 3.1 bitcast_multiply_fusion.1
  15.8 3.9 copy.51
  19.7 3.1 bitcast_multiply_fusion
  22.8 0.9 copy-done.3
  25.0 6.3 %all-to-all-start = ((bf16[64,16,128]{2,1,0:T(8,128)(2,1)}), bf16[64,16,128]{2,1,0:T(8,128)(2,1)S(1)}, u32[]{:S(2)}, u32[]{:S(2)}) async-start(bf16[64,16,128]{2,1,0:T(8,128)(2,1)} %bitcast.6), calls=%async_computation | async-start | bytes 524288 | tf_op jit(solution)/shard_map/all_to_all | solution.py:90
  31.3 142.1 %all-gather.3.cloned.1.call-done = bf16[4096,1024]{0,1:T(8,128)(2,1)} async-done(((bf16[1024,1024]{0,1:T(8,128)(2,1)}), bf16[4096,1024]{0,1:T(8,128)(2,1)}) %all-gather.3.cloned.1.call-update) | async-done | bytes 8388624 | tf_op jit(solution)/shard_map/all_gather | solution.py:68
  173.5 5.7 %fusion.21 = bf16[256,1024]{0,1:T(8,128)(2,1)S(1)} fusion(bf16[4096,1024]{0,1:T(8,128)(2,1)} %all-gather.3.cloned.1.call-done, bf16[256,4096]{1,0:T(8,128)(2,1)S(1)} %bitcast.87), kind=kOutput, calls=%fused_computation.36 | convolution fusion | flops 2147745792 | bytes 11010048 | tf_op jit(solution)/shard_map/dot_general | solution.py:44
  179.2 143.6 %all-gather.5.cloned.1.call-done = bf16[4096,1024]{0,1:T(8,128)(2,1)} async-done(((bf16[1024,1024]{0,1:T(8,128)(2,1)}), bf16[4096,1024]{0,1:T(8,128)(2,1)}) %all-gather.5.cloned.1.call-update) | async-done | bytes 8388624 | tf_op jit(solution)/shard_map/all_gather | solution.py:69
  322.9 6.5 %fusion.22 = bf16[256,1024]{0,1:T(8,128)(2,1)} fusion(bf16[4096,1024]{0,1:T(8,128)(2,1)} %all-gather.5.cloned.1.call-done, bf16[256,4096]{1,0:T(8,128)(2,1)S(1)} %bitcast.88), kind=kOutput, calls=%fused_computation.37 | convolution fusion | flops 2147745792 | bytes 11010048 | tf_op jit(solution)/shard_map/dot_general | solution.py:45
  329.4 1.4 convert_element_type.73
  330.8 1.7 copy.52
  332.6 2.8 convert_element_type.79
  335.3 2.4 copy.53
  337.7 2.8 pad_maximum_fusion
  340.6 3.5 all-to-all-start.1
  345.0 25.3 %all-to-all-done.1 = bf16[64,64,128]{2,1,0:T(8,128)(2,1)S(1)} async-done(((bf16[64,64,128]{2,1,0:T(8,128)(2,1)}), bf16[64,64,128]{2,1,0:T(8,128)(2,1)S(1)}, u32[]{:S(2)}, u32[]{:S(2)}) %all-to-all-start.1) | async-done | bytes 1048608 | tf_op jit(solution)/shard_map/all_to_all | solution.py:92
  370.3 1.1 copy.54
  371.3 83.0 %while.12 = (s32[]{:T(128)}, bf16[16,64,128]{2,1,0:T(8,128)(2,1)S(1)}, bf16[16,256,128]{1,2,0:T(8,128)(2,1)}, s32[16]{0:T(128)S(1)}, bf16[16,64,128]{2,1,0:T(8,1...) while((s32[]{:T(128)}, bf16[16,64,128]{2,1,0:T(8,128)(2,1)S(1)}, bf16[16,256,128]{1,2,0:T(8,128)(2,1)}, ...), condition=%wide.region_5.6_spmd, body=%wide.region_1.5_spmd.sunk | while | flops 13144130 | bytes 1192309 | solution.py:109
  373.3 0.8 dynamic-slice_bitcast_fusion.4
  378.5 0.8 dynamic-slice_bitcast_fusion.4
  383.7 0.8 dynamic-slice_bitcast_fusion.4
  388.9 0.8 dynamic-slice_bitcast_fusion.4
  394.1 0.8 dynamic-slice_bitcast_fusion.4
  399.3 0.8 dynamic-slice_bitcast_fusion.4
  404.4 0.8 dynamic-slice_bitcast_fusion.4
  409.6 0.8 dynamic-slice_bitcast_fusion.4
  414.8 0.8 dynamic-slice_bitcast_fusion.4
  420.0 0.8 dynamic-slice_bitcast_fusion.4
  425.2 0.8 dynamic-slice_bitcast_fusion.4
  430.3 0.8 dynamic-slice_bitcast_fusion.4
  435.5 0.8 dynamic-slice_bitcast_fusion.4
  440.7 0.8 dynamic-slice_bitcast_fusion.4
  445.9 0.8 dynamic-slice_bitcast_fusion.4
  454.3 1.9 copy.56
  456.2 27.8 %all_to_all.60 = bf16[16,256,128]{2,0,1:T(8,128)(2,1)S(1)} all-to-all(bf16[16,256,128]{2,0,1:T(8,128)(2,1)S(1)} %copy.56), channel_id=1, replica_groups=mesh['grp'=2,'seq'=4,'head'=4] {'seq'}, dimensions={1} | all-to-all | bytes 2097152 | tf_op jit(solution)/shard_map/all_to_all | solution.py:112
  484.3 1.5 fusion.25
  486.5 1.6 reshape_reshape.7
  488.0 1.9 copy.58
  489.9 1.5 reshape_reshape.6
  491.4 5.9 %fusion.27 = f32[256,4096]{1,0:T(8,128)S(1)} fusion(bf16[256,1024]{1,0:T(8,128)(2,1)} %reshape_reshape.6, bf16[4096,1024]{0,1:T(8,128)(2,1)} %all-gather.3.cloned.1.call-done), kind=kOutput, calls=%fused_computation.52 | convolution fusion | flops 2147483648 | bytes 13107200 | tf_op jit(solution)/shard_map/dot_general | solution.py:52
  497.4 7.8 %convolution_add_fusion = f32[256,4096]{1,0:T(8,128)} fusion(f32[256,4096]{1,0:T(8,128)S(1)} %fusion.27, bf16[256,1024]{1,0:T(8,128)(2,1)S(1)} %copy-done.1, bf16[4096,1024]{0,1:T(8,128)(2,1)} %all-gather.5.cloned.1.call-done), kind=kOutput, calls=%fused_computation.31 | convolution fusion | flops 2148532224 | bytes 17301504 | tf_op jit(solution)/shard_map/dot_general | solution.py:53
  505.4 10.8 %all_to_all.61 = bf16[16,64,128]{2,0,1:T(8,128)(2,1)S(1)} all-to-all(bf16[16,64,128]{2,0,1:T(8,128)(2,1)S(1)} %copy.55), channel_id=1, replica_groups=mesh['grp'=2,'seq'=4,'head'=4] {'seq'}, dimensions={1} | all-to-all | bytes 524288 | tf_op jit(solution)/shard_map/all_to_all | solution.py:111
  516.4 0.9 reshape.86
  517.2 0.9 reshape.85
  518.1 30.9 %reduce-scatter.2.cloned.1.call-done = f32[256,1024]{1,0:T(8,128)} async-done(((f32[256,4096]{1,0:T(8,128)}), f32[256,1024]{1,0:T(8,128)}) %reduce-scatter.2.cloned.1.call-update) | async-done | bytes 1048592 | tf_op jit(solution)/shard_map/reduce_scatter | solution.py:119
  549.0 2.1 convert_element_type.80
  (231 shorter events, 73.7 us)
Async XLA Ops:
  7.2 166.3 %copy-start = (bf16[4,64,4096]{2,1,0:T(8,128)(2,1)S(1)}, bf16[4,64,4096]{2,1,0:T(8,128)(2,1)}, u32[]{:S(2)}) copy-start(bf16[4,64,4096]{2,1,0:T(8,128)(2,1)} %param.9) | copy-start | bytes 6291460
  7.2 166.3 %all-gather.3.cloned.1.call-start = ((), (), s32[]{:S(2)}) async-start(), calls=%async_computation.5 | async-start | bytes 10485760 | tf_op jit(solution)/shard_map/all_gather | solution.py:68
  15.4 307.4 %all-gather.5.cloned.1.call-start = ((), (), s32[]{:S(2)}) async-start(), calls=%async_computation.6 | async-start | bytes 10485760 | tf_op jit(solution)/shard_map/all_gather | solution.py:69
  22.8 0.9 copy-start.3
  22.8 1.1 copy-start.4
  25.0 315.6 %all-to-all-start = ((bf16[64,16,128]{2,1,0:T(8,128)(2,1)}), bf16[64,16,128]{2,1,0:T(8,128)(2,1)S(1)}, u32[]{:S(2)}, u32[]{:S(2)}) async-start(bf16[64,16,128]{2,1,0:T(8,128)(2,1)} %bitcast.6), calls=%async_computation | async-start | bytes 524288 | tf_op jit(solution)/shard_map/all_to_all | solution.py:90
  337.7 6.4 %copy-start.5 = (s32[4]{0:T(128)S(1)}, s32[4]{0:T(128)}, u32[]{:S(2)}) copy-start(s32[4]{0:T(128)} %param.13) | copy-start | bytes 52
  340.6 29.7 %all-to-all-start.1 = ((bf16[64,64,128]{2,1,0:T(8,128)(2,1)}), bf16[64,64,128]{2,1,0:T(8,128)(2,1)S(1)}, u32[]{:S(2)}, u32[]{:S(2)}) async-start(bf16[64,64,128]{2,1,0:T(8,128)(2,1)} %bitcast.18), calls=%async_computation.1 | async-start | bytes 2097152 | tf_op jit(solution)/shard_map/all_to_all | solution.py:92
  344.1 204.9 %reduce-scatter.2.cloned.1.call-start = ((), (), s32[]{:S(2)}) async-start(), calls=%async_computation.7 | async-start | bytes 5242880 | tf_op jit(solution)/shard_map/reduce_scatter | solution.py:119
  345.0 26.3 %copy-start.2 = (bf16[16,64,128]{2,1,0:T(8,128)(2,1)S(1)}, bf16[16,64,128]{2,1,0:T(8,128)(2,1)}, u32[]{:S(2)}) copy-start(bf16[16,64,128]{2,1,0:T(8,128)(2,1)} %custom-call) | copy-start | bytes 786436
  491.4 6.0 %copy-start.1 = (bf16[256,1024]{1,0:T(8,128)(2,1)S(1)}, bf16[256,1024]{1,0:T(8,128)(2,1)}, u32[]{:S(2)}) copy-start(bf16[256,1024]{1,0:T(8,128)(2,1)} %reshape_reshape.7) | copy-start | bytes 1572868
Sparse Core Ops, SparseCore 0:
  15.5 157.8 all-gather.2
  175.1 147.7 all-gather.4
  505.4 43.5 reduce-scatter.1
where the time goes:
time: 560 us; the launch traced here: 558 us
  waiting for transfers between devices  342 us (61%)
  local copies, waits for them, and re-layouts  66.4 us (12%)
  matrix products  48.8 us (9%)
  blocking collectives  38.6 us (7%)
  other arithmetic  37.3 us (7%)
  between operations  13.9 us (2%)
  starting transfers between devices  9.98 us (2%)
    all_gather x1, waiting for transfers between devices, body(): lax.all_gather(value_masked, 'seq', axis=0, tiled=True)  144 us
    all_gather x1, waiting for transfers between devices, body(): lax.all_gather(key_masked, 'seq', axis=0, tiled=True)  142 us
    reduce_scatter x1, waiting for transfers between devices, body(): lax.psum_scatter(grad_terms, 'head', scatter_dimension=1, tiled=True)  30.9 us
    all_to_all x1, blocking collectives, body(): lax.all_to_all(back, 'seq', split_axis=1, concat_axis=0, tiled=True)  27.8 us
    all_to_all x1, waiting for transfers between devices, body(): lax.all_to_all(kv_pairs, 'seq', split_axis=0, concat_axis=1, tiled=True)  25.3 us
    squeeze x32, local copies, waits for them, and re-layouts, body(): front, back = lax.map(owner_pair, (kv_owned, query_owned, pair_length))  25.1 us
    dynamic_update_slice x32, other arithmetic, body(): front, back = lax.map(owner_pair, (kv_owned, query_owned, pair_length))  11.7 us
  transfers between devices with their start and end apart: 5, of which 4 were waited for; matrix products, arithmetic and copies ran while one was open for 6% of the time, Pallas kernels for 0%

commit v1 on v0

--- a/solution.py
+++ b/solution.py
@@ -8,6 +8,22 @@
 DOCS = 4
 SCALE = 0.125
 FLOOR_SCORE = -1e30
+
+
+def collect(x, axis, dim):
+    ways, here, step = (lax.axis_size(axis), lax.axis_index(axis), x.shape[dim])
+    shape = [n * ways if d == dim else n for d, n in enumerate(x.shape)]
+    full = lax.dynamic_update_slice_in_dim(jnp.zeros(shape, x.dtype), x, here * step, axis=dim)
+    going_up = going_down = x
+    for far in range(1, ways // 2 + 1):
+        going_up = lax.ppermute(going_up, axis, [(d, (d + 1) % ways) for d in range(ways)])
+        full = lax.dynamic_update_slice_in_dim(full, going_up, (here - far) % ways * step, axis=dim)
+        if 2 * far < ways:
+            going_down = lax.ppermute(going_down, axis, [(d, (d - 1) % ways) for d in range(ways)])
+            full = lax.dynamic_update_slice_in_dim(
+                full, going_down, (here + far) % ways * step, axis=dim
+            )
+    return full
 
 
 def expand(tile_grid, tile_edge):
@@ -65,7 +81,7 @@
     key_masked = key_weight * expand(tile_mask[0], TILE).astype(jnp.bfloat16)
     value_masked = value_weight * expand(tile_mask[1], TILE).astype(jnp.bfloat16)
     full_key, full_value = (
-        lax.all_gather(key_masked, "seq", axis=0, tiled=True),
+        collect(key_masked, "seq", 0),
         lax.all_gather(value_masked, "seq", axis=0, tiled=True),
     )
     key_sum, value_sum = project(encoder, full_key, full_value)

time: 560 us -> 524 us (0.936)
  waiting for transfers between devices: 342 us -> 223 us
  starting transfers between devices: 9.98 us -> 102 us
  local copies, waits for them, and re-layouts: 66.4 us -> 58.7 us
    ppermute x0 -> x3, waiting for transfers between devices: none -> 170 us  [the longest x2 170 us: collect(): lax.ppermute(going_up, axis, [(d, (d + 1) % ways) for d in range(ways)])]
    all_gather x1, waiting for transfers between devices: 144 us -> 0.02 us  [body(): lax.all_gather(value_masked, 'seq', axis=0, tiled=True)]
    all_gather x1 -> x0, waiting for transfers between devices: 142 us -> none  [body(): lax.all_gather(key_masked, 'seq', axis=0, tiled=True)]
    ppermute x0 -> x3, starting transfers between devices: none -> 88.7 us  [the longest x2 86.5 us: collect(): lax.ppermute(going_up, axis, [(d, (d + 1) % ways) for d in range(ways)])]
    squeeze x32, local copies, waits for them, and re-layouts: 25.1 us -> 11.7 us  [body(): front, back = lax.map(owner_pair, (kv_owned, query_owned, pair_length))]
    dynamic_update_slice x0 -> x3, local copies, waits for them, and re-layouts: none -> 9.34 us  [the longest x2 6.25 us: collect(): lax.dynamic_update_slice_in_dim(full, going_up, (here - far) % ways * ste...]
  transfers between devices with their start and end apart: 5 -> 7, of which waited for: 4 -> 4; matrix products, arithmetic and copies ran while one was open for 6% -> 9% of each run, Pallas kernels for 0% -> 0%
where the time goes in v1:
time: 524 us; the launch traced here: 522 us
  waiting for transfers between devices  223 us (43%)
  starting transfers between devices  102 us (19%)
  local copies, waits for them, and re-layouts  58.7 us (11%)
  matrix products  48.4 us (9%)
  blocking collectives  38.6 us (7%)
  other arithmetic  35.6 us (7%)
  between operations  14.3 us (3%)
    ppermute x2, waiting for transfers between devices, collect(): lax.ppermute(going_up, axis, [(d, (d + 1) % ways) for d in range(ways)])  170 us
    ppermute x2, starting transfers between devices, collect(): lax.ppermute(going_up, axis, [(d, (d + 1) % ways) for d in range(ways)])  86.5 us
    reduce_scatter x1, waiting for transfers between devices, body(): lax.psum_scatter(grad_terms, 'head', scatter_dimension=1, tiled=True)  29.8 us
    all_to_all x1, blocking collectives, body(): lax.all_to_all(back, 'seq', split_axis=1, concat_axis=0, tiled=True)  27.7 us
    all_to_all x1, waiting for transfers between devices, body(): lax.all_to_all(kv_pairs, 'seq', split_axis=0, concat_axis=1, tiled=True)  23.6 us
    squeeze x32, local copies, waits for them, and re-layouts, body(): front, back = lax.map(owner_pair, (kv_owned, query_owned, pair_length))  11.7 us
    dynamic_update_slice x32, other arithmetic, body(): front, back = lax.map(owner_pair, (kv_owned, query_owned, pair_length))  11.4 us
    all_to_all x1, blocking collectives, body(): lax.all_to_all(front, 'seq', split_axis=1, concat_axis=0, tiled=True)  10.9 us
  transfers between devices with their start and end apart: 7, of which 4 were waited for; matrix products, arithmetic and copies ran while one was open for 9% of the time, Pallas kernels for 0%

profile of v1, /device:TPU:0, one launch (start us, length us, event | category | flops | bytes accessed | tf_op | source)
XLA Modules:
  0.0 522.2 jit_solution(1714573954453987035)
XLA Ops:
  7.2 0.9 convert.4
  8.4 4.0 copy.51
  12.4 3.1 bitcast_multiply_fusion
  15.8 3.9 copy.49
  19.8 4.3 broadcast_in_dim.70
  24.0 2.9 constant_dynamic-update-slice_fusion.3
  26.9 3.0 collective-permute-start
  29.9 2.2 collective-permute-start.1
  32.1 91.5 %collective-permute-done = bf16[1024,1024]{0,1:T(8,128)(2,1)} collective-permute-done((bf16[1024,1024]{0,1:T(8,128)(2,1)}, bf16[1024,1024]{0,1:T(8,128)(2,1)}, u32[]{:S(2)}, u32[]{:S(2)}) %collective-permute-start) | collective-permute-done | bytes 2097184 | tf_op jit(solution)/shard_map/ppermute | solution.py:19
  123.6 83.6 %collective-permute-start.2 = (bf16[1024,1024]{0,1:T(8,128)(2,1)}, bf16[1024,1024]{0,1:T(8,128)(2,1)}, u32[]{:S(2)}, u32[]{:S(2)}) collective-permute-start(bf16[1024,1024]{0,1:T(8,128)(2,1)} %collective-permute-done), channel_id=1, source_target_pairs={{0,4},{4,8},{8,12},{12,0},{1,5},{5,9},{9,13},{13,1},{2,6},{6,10},{... | collective-permute-start | bytes 6291464 | tf_op jit(solution)/shard_map/ppermute | solution.py:19
  207.7 0.8 copy.46
  208.5 9.9 %all-to-all-start = ((bf16[64,16,128]{2,1,0:T(8,128)(2,1)}), bf16[64,16,128]{2,1,0:T(8,128)(2,1)S(1)}, u32[]{:S(2)}, u32[]{:S(2)}) async-start(bf16[64,16,128]{2,1,0:T(8,128)(2,1)} %bitcast.6), calls=%async_computation | async-start | bytes 524288 | tf_op jit(solution)/shard_map/all_to_all | solution.py:106
  218.4 3.2 constant_dynamic-update-slice_fusion.2
  221.6 3.1 constant_dynamic-update-slice_fusion.1
  224.7 78.2 %collective-permute-done.2 = bf16[1024,1024]{0,1:T(8,128)(2,1)} collective-permute-done((bf16[1024,1024]{0,1:T(8,128)(2,1)}, bf16[1024,1024]{0,1:T(8,128)(2,1)}, u32[]{:S(2)}, u32[]{:S(2)}) %collective-permute-start.2) | collective-permute-done | bytes 2097184 | tf_op jit(solution)/shard_map/ppermute | solution.py:19
  302.9 3.1 constant_dynamic-update-slice_fusion
  306.0 5.8 %fusion.21 = bf16[256,1024]{0,1:T(8,128)(2,1)S(1)} fusion(bf16[4096,1024]{0,1:T(8,128)(2,1)} %constant_dynamic-update-slice_fusion, bf16[256,4096]{1,0:T(8,128)(2,1)S(1)} %bitcast.87), kind=kOutput, calls=%fused_computation.36 | convolution fusion | flops 2147745792 | bytes 11010048 | tf_op jit(solution)/shard_map/dot_general | solution.py:60
  311.8 1.4 convert_element_type.73
  313.2 1.7 copy.52
  314.9 6.5 %fusion.22 = bf16[256,1024]{0,1:T(8,128)(2,1)} fusion(bf16[4096,1024]{0,1:T(8,128)(2,1)} %all-gather.2.cloned.1.call-done, bf16[256,4096]{1,0:T(8,128)(2,1)S(1)} %bitcast.88), kind=kOutput, calls=%fused_computation.37 | convolution fusion | flops 2147745792 | bytes 11010048 | tf_op jit(solution)/shard_map/dot_general | solution.py:61
  321.5 2.0 convert_element_type.79
  323.5 0.8 copy.53
  324.3 1.6 pad_maximum_fusion
  325.9 3.5 all-to-all-start.1
  329.8 0.7 copy.47
  330.5 23.6 %all-to-all-done.1 = bf16[64,64,128]{2,1,0:T(8,128)(2,1)S(1)} async-done(((bf16[64,64,128]{2,1,0:T(8,128)(2,1)}), bf16[64,64,128]{2,1,0:T(8,128)(2,1)S(1)}, u32[]{:S(2)}, u32[]{:S(2)}) %all-to-all-start.1) | async-done | bytes 1048608 | tf_op jit(solution)/shard_map/all_to_all | solution.py:108
  354.2 69.4 %while.12 = (s32[]{:T(128)}, bf16[16,64,128]{2,1,0:T(8,128)(2,1)}, bf16[16,256,128]{1,2,0:T(8,128)(2,1)S(1)}, s32[16]{0:T(128)S(1)}, bf16[16,64,128]{2,1,0:T(8,1...) while((s32[]{:T(128)}, bf16[16,64,128]{2,1,0:T(8,128)(2,1)}, bf16[16,256,128]{1,2,0:T(8,128)(2,1)S(1)}, ...), condition=%wide.region_5.6_spmd, body=%wide.region_1.5_spmd.sunk | while | flops 13144130 | bytes 1176425 | solution.py:125
  354.2 0.7 dynamic-slice_bitcast_fusion.5
  358.6 0.7 dynamic-slice_bitcast_fusion.5
  362.9 0.7 dynamic-slice_bitcast_fusion.5
  367.2 0.7 dynamic-slice_bitcast_fusion.5
  371.6 0.7 dynamic-slice_bitcast_fusion.5
  375.9 0.7 dynamic-slice_bitcast_fusion.5
  380.2 0.7 dynamic-slice_bitcast_fusion.5
  384.6 0.7 dynamic-slice_bitcast_fusion.5
  388.9 0.7 dynamic-slice_bitcast_fusion.5
  393.2 0.7 dynamic-slice_bitcast_fusion.5
  397.6 0.7 dynamic-slice_bitcast_fusion.5
  423.6 1.1 copy.56
  424.7 27.7 %all_to_all.60 = bf16[16,256,128]{2,0,1:T(8,128)(2,1)S(1)} all-to-all(bf16[16,256,128]{2,0,1:T(8,128)(2,1)S(1)} %copy.56), channel_id=1, replica_groups=mesh['grp'=2,'seq'=4,'head'=4] {'seq'}, dimensions={1} | all-to-all | bytes 2097152 | tf_op jit(solution)/shard_map/all_to_all | solution.py:128
  456.0 5.7 %fusion.27 = f32[256,4096]{1,0:T(8,128)S(1)} fusion(bf16[256,1024]{1,0:T(8,128)(2,1)S(1)} %reshape_reshape.7, bf16[4096,1024]{0,1:T(8,128)(2,1)} %all-gather.2.cloned.1.call-done), kind=kOutput, calls=%fused_computation.56 | convolution fusion | flops 2147483648 | bytes 13107200 | tf_op jit(solution)/shard_map/dot_general | solution.py:69
  461.7 7.8 %convolution_add_fusion = f32[256,4096]{1,0:T(8,128)} fusion(f32[256,4096]{1,0:T(8,128)S(1)} %fusion.27, bf16[256,1024]{1,0:T(8,128)(2,1)S(1)} %reshape_reshape.6, bf16[4096,1024]{0,1:T(8,128)(2,1)} %constant_dynamic-update-slice_fusion), kind=kOutput, calls=%fused_computation.31 | convolution fusion | flops 2148532224 | bytes 17301504 | tf_op jit(solution)/shard_map/dot_general | solution.py:68
  469.5 0.9 copy-done.3
  470.6 10.9 %all_to_all.61 = bf16[16,64,128]{2,0,1:T(8,128)(2,1)S(1)} all-to-all(bf16[16,64,128]{2,0,1:T(8,128)(2,1)S(1)} %copy.55), channel_id=1, replica_groups=mesh['grp'=2,'seq'=4,'head'=4] {'seq'}, dimensions={1} | all-to-all | bytes 524288 | tf_op jit(solution)/shard_map/all_to_all | solution.py:127
  481.7 0.9 reshape.85
  482.5 0.9 reshape.86
  483.4 29.8 %reduce-scatter.2.cloned.1.call-done = f32[256,1024]{1,0:T(8,128)} async-done(((f32[256,4096]{1,0:T(8,128)}), f32[256,1024]{1,0:T(8,128)}) %reduce-scatter.2.cloned.1.call-update) | async-done | bytes 1048592 | tf_op jit(solution)/shard_map/reduce_scatter | solution.py:135
  513.2 2.1 convert_element_type.80
  (240 shorter events, 66.1 us)
Async XLA Ops:
  7.2 298.8 %copy-start = (bf16[4,64,4096]{2,1,0:T(8,128)(2,1)S(1)}, bf16[4,64,4096]{2,1,0:T(8,128)(2,1)}, u32[]{:S(2)}) copy-start(bf16[4,64,4096]{2,1,0:T(8,128)(2,1)} %param.9) | copy-start | bytes 6291460
  7.2 307.7 %all-gather.2.cloned.1.call-start = ((), (), s32[]{:S(2)}) async-start(), calls=%async_computation.5 | async-start | bytes 10485760 | tf_op jit(solution)/shard_map/all_gather | solution.py:85
  19.7 4.3 copy-start.2
  24.0 183.1 %copy-start.4 = (bf16[4,16,1024]{2,1,0:T(8,128)(2,1)S(1)}, bf16[4,16,1024]{2,1,0:T(8,128)(2,1)}, u32[]{:S(2)}) copy-start(bf16[4,16,1024]{2,1,0:T(8,128)(2,1)} %param.14) | copy-start | bytes 393220
  24.0 183.3 %copy-start.5 = (bf16[4,16,1024]{2,1,0:T(8,128)(2,1)S(1)}, bf16[4,16,1024]{2,1,0:T(8,128)(2,1)}, u32[]{:S(2)}) copy-start(bf16[4,16,1024]{2,1,0:T(8,128)(2,1)} %param.15) | copy-start | bytes 393220
  26.9 96.6 %collective-permute-start = (bf16[1024,1024]{0,1:T(8,128)(2,1)}, bf16[1024,1024]{0,1:T(8,128)(2,1)}, u32[]{:S(2)}, u32[]{:S(2)}) collective-permute-start(bf16[1024,1024]{0,1:T(8,128)(2,1)} %get-tuple-element.61), channel_id=1, source_target_pairs={{0,4},{4,8},{8,12},{12,0},{1,5},{5,9},{9,13},{13,1},{2,6},{6,10},{... | collective-permute-start | bytes 6291464 | tf_op jit(solution)/shard_map/ppermute | solution.py:19
  29.9 191.7 %collective-permute-start.1 = (bf16[1024,1024]{0,1:T(8,128)(2,1)}, bf16[1024,1024]{0,1:T(8,128)(2,1)}, u32[]{:S(2)}, u32[]{:S(2)}) collective-permute-start(bf16[1024,1024]{0,1:T(8,128)(2,1)} %get-tuple-element.61), channel_id=1, source_target_pairs={{0,12},{4,0},{8,4},{12,8},{1,13},{5,1},{9,5},{13,9},{2,14},{6,2},{... | collective-permute-start | bytes 6291464 | tf_op jit(solution)/shard_map/ppermute | solution.py:22
  123.6 179.3 %collective-permute-start.2 = (bf16[1024,1024]{0,1:T(8,128)(2,1)}, bf16[1024,1024]{0,1:T(8,128)(2,1)}, u32[]{:S(2)}, u32[]{:S(2)}) collective-permute-start(bf16[1024,1024]{0,1:T(8,128)(2,1)} %collective-permute-done), channel_id=1, source_target_pairs={{0,4},{4,8},{8,12},{12,0},{1,5},{5,9},{9,13},{13,1},{2,6},{6,10},{... | collective-permute-start | bytes 6291464 | tf_op jit(solution)/shard_map/ppermute | solution.py:19
  208.5 117.4 %all-to-all-start = ((bf16[64,16,128]{2,1,0:T(8,128)(2,1)}), bf16[64,16,128]{2,1,0:T(8,128)(2,1)S(1)}, u32[]{:S(2)}, u32[]{:S(2)}) async-start(bf16[64,16,128]{2,1,0:T(8,128)(2,1)} %bitcast.6), calls=%async_computation | async-start | bytes 524288 | tf_op jit(solution)/shard_map/all_to_all | solution.py:106
  321.5 8.2 %copy-start.6 = (s32[4]{0:T(128)S(1)}, s32[4]{0:T(128)}, u32[]{:S(2)}) copy-start(s32[4]{0:T(128)} %param.13) | copy-start | bytes 52
  325.9 28.2 %all-to-all-start.1 = ((bf16[64,64,128]{2,1,0:T(8,128)(2,1)}), bf16[64,64,128]{2,1,0:T(8,128)(2,1)S(1)}, u32[]{:S(2)}, u32[]{:S(2)}) async-start(bf16[64,64,128]{2,1,0:T(8,128)(2,1)} %bitcast.18), calls=%async_computation.1 | async-start | bytes 2097152 | tf_op jit(solution)/shard_map/all_to_all | solution.py:108
  329.4 183.8 %reduce-scatter.2.cloned.1.call-start = ((), (), s32[]{:S(2)}) async-start(), calls=%async_computation.6 | async-start | bytes 5242880 | tf_op jit(solution)/shard_map/reduce_scatter | solution.py:135
  469.5 0.9 copy-start.3
  469.5 45.8 %copy-start.1 = (bf16[4,64,4096]{2,1,0:T(8,128)(2,1)S(1)}, bf16[4,64,4096]{2,1,0:T(8,128)(2,1)}, u32[]{:S(2)}) copy-start(bf16[4,64,4096]{2,1,0:T(8,128)(2,1)} %param.9) | copy-start | bytes 6291460
Sparse Core Ops, SparseCore 0:
  15.6 292.2 all-gather.1
  469.7 43.5 reduce-scatter.1
